TPU v7x, 128 devices: a whole 4x4x4 slice. The times are simulated.
128 devices in a mesh: frames: 16 (over x, y_lo, core), pairs: 8 (over y_hi, z).
Axes of the slice: x: 4, y: 4 (y_hi: 2, y_lo: 2; y = y_hi * 2 + y_lo), z: 4, core: 2. Of those that a mesh axis runs over, the one named last changes fastest.
Arguments:
- coords: float32 [8192, 3, 384], P('frames'), may hold values from -3 to 3
- pair_first: int32 [512], P('pairs'), may hold values from 0 to 383
- pair_second: int32 [65536], P('pairs'), may hold values from 0 to 383
- enc_weight: bfloat16 [64, 65536], P(None, 'pairs'), may hold values from -0.0234375 to 0.0234375
- enc_bias: float32 [64], replicated, may hold values from -4 to 4
- dec_weight: bfloat16 [64, 65536], P(None, 'pairs'), may hold values from -0.75 to 0.75
- dec_bias: float32 [65536], P('pairs'), may hold values from -3 to 3
- lag_frames: int32 [1], replicated, may hold values from 256 to 512
Outputs:
- grad_enc: float32 [64, 65536], P(None, 'pairs')
- grad_dec: float32 [64, 65536], P(None, 'pairs')
Inputs may be any that keep to these rules, and one draw needn't show every extreme that they name: Residue numbers; pair p joins residue pair_first[p // 128] with residue pair_second[p].
All inputs are finite; a program needn't handle non-finite values.
Results may differ from a plain program's by a relative error of at most 0.0003.
Values may be sent and summed in bfloat16 or wider, within the bound.
No kernel may reach another device: no remote copies, remote signals or barrier semaphores. Data moves between devices by JAX's collectives and lax.ppermute only.
A program may use at most 192 MiB of HBM per device.

v0:
```python
from functools import partial
import jax
import jax.numpy as jnp
from jax import lax
from jax.sharding import PartitionSpec as P

cutoff_dist = 2.3
softness = 0.4


def from_behind(block, axis, distance):
    devices = range(lax.axis_size(axis))
    route = [(i - distance, i) for i in devices if i - distance in devices]
    return lax.ppermute(block, axis, route)


def contact_rows(frame_block, first_res, second):
    near = jnp.take(frame_block, first_res, axis=2)
    far = jnp.take(frame_block, second, axis=2)
    far = far.reshape(far.shape[0], 3, first_res.shape[0], 128)
    offset = far - near[..., None]
    distance = jnp.sqrt(jnp.sum(offset * offset, axis=1))
    value = jax.nn.sigmoid((cutoff_dist - distance) / softness)
    return value.reshape(frame_block.shape[0], -1).astype(jnp.bfloat16)


def all_contacts(coords, first_res, second):
    frame_rows = coords.shape[0]
    block_rows = min(128, frame_rows)
    grouped = coords.reshape(frame_rows // block_rows, block_rows, coords.shape[1], coords.shape[2])
    result = lax.map(partial(contact_rows, first_res=first_res, second=second), grouped)
    return result.reshape(frame_rows, -1)


def later_rows(own, following, row_ids, frame_rows):
    own_part = jnp.take(own, jnp.minimum(row_ids, frame_rows - 1), axis=0)
    next_part = jnp.take(following, jnp.maximum(row_ids - frame_rows, 0), axis=0)
    inside = (row_ids < frame_rows).reshape((-1,) + (1,) * (own.ndim - 1))
    return jnp.where(inside, own_part, next_part)


def local(coords, pair_first, pair_second, enc_weight, enc_bias, dec_weight, dec_bias, lag_frames):
    frame_rows = coords.shape[0]
    total_frames = frame_rows * lax.axis_size("frames")
    shift_now = lag_frames[0]
    own_contacts = all_contacts(coords, pair_first, pair_second)
    following = from_behind(own_contacts, "frames", -1)
    partial_sum = lax.dot_general(
        enc_weight, own_contacts, (((1,), (1,)), ((), ())), preferred_element_type=jnp.float32
    )
    latent = jnp.tanh(lax.psum(partial_sum, "pairs") + enc_bias[:, None])
    latent_bf = latent.astype(jnp.bfloat16)
    scale_factor = 1.0 / jnp.sqrt(jnp.float32(total_frames) - shift_now.astype(jnp.float32))
    block_rows = min(512, frame_rows)
    block_count = frame_rows // block_rows
    first_frame = lax.axis_index("frames") * frame_rows

    def decode_block(grad_sum, block_idx):
        begin_row = block_idx * block_rows
        local_ids = begin_row + jnp.arange(block_rows, dtype=jnp.int32)
        row_ids = local_ids + shift_now
        target = later_rows(own_contacts, following, row_ids, frame_rows)
        decoded = (
            lax.dot_general(
                latent_bf, dec_weight, (((0,), (0,)), ((), ())), preferred_element_type=jnp.float32
            )
            + dec_bias[None, :]
        )
        usable = first_frame + local_ids + shift_now < total_frames
        err_bf = jnp.where(
            usable[:, None], (decoded - target.astype(jnp.float32)) * scale_factor, 0.0
        ).astype(jnp.bfloat16)
        grad_sum = grad_sum + jnp.dot(latent_bf, err_bf, preferred_element_type=jnp.float32)
        back_block = lax.dot_general(
            dec_weight, err_bf, (((1,), (1,)), ((), ())), preferred_element_type=jnp.float32
        )
        return (grad_sum, back_block)

    zeros = jnp.zeros((latent.shape[0], dec_weight.shape[1]), jnp.float32)
    grad_dec, back_blocks = lax.scan(decode_block, zeros, jnp.arange(block_count, dtype=jnp.int32))
    back_terms = jnp.transpose(back_blocks, (1, 0, 2)).reshape(latent.shape[0], frame_rows)
    backward = lax.psum(back_terms, "pairs")
    hidden_bf = (backward * (1.0 - latent * latent)).astype(jnp.bfloat16)
    grad_enc = jnp.dot(hidden_bf, own_contacts, preferred_element_type=jnp.float32)
    grad_dec, grad_enc = lax.psum((grad_dec, grad_enc), "frames")
    return (grad_enc, grad_dec)


def solution(mesh):
    placed = (
        P("frames", None, None),
        P("pairs"),
        P("pairs"),
        P(None, "pairs"),
        P(),
        P(None, "pairs"),
        P("pairs"),
        P(),
    )
    return jax.shard_map(
        local,
        mesh=mesh,
        in_specs=placed,
        out_specs=(P(None, "pairs"), P(None, "pairs")),
        check_vma=False,
    )
```

profile of v0, /device:TPU:0, one launch (start us, length us, event | category | flops | bytes accessed | tf_op | source)
XLA Modules:
  0.0 823.3 jit_solution(3909381968403380009)
XLA Ops:
  7.2 363.3 %while.2 = (s32[]{:T(128)}, bf16[4,128,8192]{2,1,0:T(8,128)(2,1)}, s32[8192]{0:T(1024)}, f32[4,128,3,384]{3,1,0,2:T(8,128)}, s32[64]{0:T(128)}, /*index=5*/s32[]{:T(128)}) while((s32[]{:T(128)}, bf16[4,128,8192]{2,1,0:T(8,128)(2,1)}, s32[8192]{0:T(1024)}, f32[4,128,3,384]{3,1,0,2:T(8,128)}, s32[64]{0:T(128)}, /*index=5*/s32[]{:T(128)}) %tuple.40), condition=%wide.region_2.3_spmd, body=%wide.region_0.2_spmd.sunk | while | flops 17933888 | bytes 85054936 | solution.py:31
  9.4 0.8 compare_select_fusion.6
  10.2 1.1 constant_dynamic-slice_fusion.2
  12.5 59.9 %gather_fusion = f32[8192,128,3]{1,2,0:T(4,128)} fusion(f32[128,3,384]{0,1,2:T(4,128)S(1)} %bitcast.54, s32[8192]{0:T(1024)S(1)} %broadcast_clamp_fusion.2), kind=kCustom, calls=%fused_computation.clone.1 | custom fusion | bytes 25198592 | tf_op jit(solution)/shard_map/while/body/eval_jaxpr/jit(_take)/gather | solution.py:19
  72.4 11.1 %copy.28 = f32[128,3,8192]{0,2,1:T(8,128)} copy(f32[128,3,8192]{0,1,2:T(4,128)} %bitcast.55) | data formatting | bytes 25165824 | tf_op jit(solution)/shard_map/while/body/eval_jaxpr/jit(_take)/gather | solution.py:19
  83.5 6.6 multiply_reduce_fusion.2
  90.1 2.0 divide_convert_fusion.2
  92.1 2.9 copy.30
  95.0 3.1 constant_dynamic-update-slice_fusion.2
  100.3 0.8 compare_select_fusion.6
  101.1 1.1 constant_dynamic-slice_fusion.2
  103.3 59.9 %gather_fusion = f32[8192,128,3]{1,2,0:T(4,128)} fusion(f32[128,3,384]{0,1,2:T(4,128)S(1)} %bitcast.54, s32[8192]{0:T(1024)S(1)} %broadcast_clamp_fusion.2), kind=kCustom, calls=%fused_computation.clone.1 | custom fusion | bytes 25198592 | tf_op jit(solution)/shard_map/while/body/eval_jaxpr/jit(_take)/gather | solution.py:19
  163.2 11.1 %copy.28 = f32[128,3,8192]{0,2,1:T(8,128)} copy(f32[128,3,8192]{0,1,2:T(4,128)} %bitcast.55) | data formatting | bytes 25165824 | tf_op jit(solution)/shard_map/while/body/eval_jaxpr/jit(_take)/gather | solution.py:19
  174.3 6.6 multiply_reduce_fusion.2
  180.9 2.0 divide_convert_fusion.2
  183.0 2.9 copy.30
  185.9 3.1 constant_dynamic-update-slice_fusion.2
  191.0 0.8 compare_select_fusion.6
  191.9 1.1 constant_dynamic-slice_fusion.2
  194.1 59.9 %gather_fusion = f32[8192,128,3]{1,2,0:T(4,128)} fusion(f32[128,3,384]{0,1,2:T(4,128)S(1)} %bitcast.54, s32[8192]{0:T(1024)S(1)} %broadcast_clamp_fusion.2), kind=kCustom, calls=%fused_computation.clone.1 | custom fusion | bytes 25198592 | tf_op jit(solution)/shard_map/while/body/eval_jaxpr/jit(_take)/gather | solution.py:19
  254.0 11.1 %copy.28 = f32[128,3,8192]{0,2,1:T(8,128)} copy(f32[128,3,8192]{0,1,2:T(4,128)} %bitcast.55) | data formatting | bytes 25165824 | tf_op jit(solution)/shard_map/while/body/eval_jaxpr/jit(_take)/gather | solution.py:19
  265.1 6.6 multiply_reduce_fusion.2
  271.7 2.0 divide_convert_fusion.2
  273.7 2.9 copy.30
  276.6 3.1 constant_dynamic-update-slice_fusion.2
  281.9 0.8 compare_select_fusion.6
  282.7 1.1 constant_dynamic-slice_fusion.2
  284.9 59.9 %gather_fusion = f32[8192,128,3]{1,2,0:T(4,128)} fusion(f32[128,3,384]{0,1,2:T(4,128)S(1)} %bitcast.54, s32[8192]{0:T(1024)S(1)} %broadcast_clamp_fusion.2), kind=kCustom, calls=%fused_computation.clone.1 | custom fusion | bytes 25198592 | tf_op jit(solution)/shard_map/while/body/eval_jaxpr/jit(_take)/gather | solution.py:19
  344.8 11.1 %copy.28 = f32[128,3,8192]{0,2,1:T(8,128)} copy(f32[128,3,8192]{0,1,2:T(4,128)} %bitcast.55) | data formatting | bytes 25165824 | tf_op jit(solution)/shard_map/while/body/eval_jaxpr/jit(_take)/gather | solution.py:19
  355.9 6.6 multiply_reduce_fusion.2
  362.5 2.0 divide_convert_fusion.2
  364.6 2.9 copy.30
  367.5 3.1 constant_dynamic-update-slice_fusion.2
  370.5 1.3 collective-permute-start
  371.8 6.9 convolution_bitcast_fusion.1
  379.8 19.9 %gather_fusion.2 = bf16[512,8192]{1,0:T(8,128)(2,1)} fusion(bf16[512,8192]{1,0:T(8,128)(2,1)} %bitcast.59, s32[1024]{0:T(1024)S(1)} %pad_clamp_fusion.2), kind=kCustom, calls=%fused_computation.2.clone | custom fusion | bytes 16779264 | tf_op jit(solution)/shard_map/while/body/eval_jaxpr/jit(_take)/gather | solution.py:36
  399.7 142.4 %all-reduce.5.cloned.1.call-done = f32[64,512]{1,0:T(8,128)} async-done(((f32[64,512]{1,0:T(8,128)}), f32[64,512]{1,0:T(8,128)}) %all-reduce.5.cloned.1.call-update) | async-done | bytes 131088 | tf_op jit(solution)/shard_map/psum | solution.py:51
  542.2 9.1 %fusion.9 = f32[512,8192]{1,0:T(8,128)} fusion(bf16[64,8192]{1,0:T(8,128)(2,1)S(1)} %copy-done, f32[64,512]{1,0:T(8,128)} %all-reduce.5.cloned.1.call-done, f32[64]{0:T(128)S(1)} %copy-done.4), kind=kOutput, calls=%fused_computation.39 | convolution fusion | flops 536936448 | bytes 17957120 | tf_op jit(solution)/shard_map/while/body/eval_jaxpr/dot_general | solution.py:64
  551.2 20.1 %gather_fusion.3 = bf16[512,8192]{1,0:T(8,128)(2,1)} fusion(bf16[512,8192]{1,0:T(8,128)(2,1)} %collective-permute-done, s32[1024]{0:T(1024)S(1)} %pad_clamp_fusion.1), kind=kCustom, calls=%fused_computation.3.clone | custom fusion | bytes 16779264 | tf_op jit(solution)/shard_map/while/body/eval_jaxpr/jit(_take)/gather | solution.py:37
  571.4 14.2 %select_convert_fusion = bf16[512,8192]{1,0:T(8,128)(2,1)S(1)} fusion(f32[512,8192]{1,0:T(8,128)} %fusion.9, bf16[512,8192]{1,0:T(8,128)(2,1)} %gather_fusion.3, bf16[512,8192]{1,0:T(8,128)(2,1)} %gather_fusion.2, f32[]{:T(128)S(6)} %sqrt.15, f32[8192]{0:T(1024)S(1)} %copy-done.3, pred[512]{0:T(512)(128)(4,1)S(1)} %get-tuple-element.89, ...), kind=kLoop, calls=%fused_computation.18 | loop fusion | flops 37748736 | bytes 41977860 | tf_op jit(solution)/shard_map/while/body/eval_jaxpr/convert_element_type | solution.py:72
  585.6 3.2 copy-done.1
  588.8 3.3 convolution_bitcast_fusion
  592.4 6.3 fusion.7
  598.8 76.2 %all-reduce.7.cloned.1.call-done = f32[64,512]{1,0:T(8,128)} async-done(((f32[64,512]{1,0:T(8,128)}), f32[64,512]{1,0:T(8,128)}) %all-reduce.7.cloned.1.call-update) | async-done | bytes 131088 | tf_op jit(solution)/shard_map/psum | solution.py:82
  675.0 6.4 fusion.2
  681.4 129.2 %all-reduce.9.cloned.1.call-done = (f32[64,8192]{1,0:T(8,128)}, f32[64,8192]{1,0:T(8,128)}) async-done(((f32[64,8192]{1,0:T(8,128)}, f32[64,8192]{1,0:T(8,128)}), (f32[64,8192]{1,0:T(8,128)}, f32[64,8192]{1,0:T(8,128)})) %all-reduce.9.cloned.1.call-update) | async-done | bytes 4194320 | tf_op jit(solution)/shard_map/psum | solution.py:85
  810.6 3.1 copy.45
  813.7 3.1 copy.46
  (59 shorter events, 13.6 us)
Async XLA Ops:
  7.2 535.0 %copy-start = (bf16[64,8192]{1,0:T(8,128)(2,1)S(1)}, bf16[64,8192]{1,0:T(8,128)(2,1)}, u32[]{:S(2)}) copy-start(bf16[64,8192]{1,0:T(8,128)(2,1)} %param.17) | copy-start | bytes 3145732
  7.2 535.0 %all-reduce.5.cloned.1.call-start = ((), (), s32[]{:S(2)}) async-start(), calls=%async_computation | async-start | bytes 262144 | tf_op jit(solution)/shard_map/psum | solution.py:51
  370.5 180.7 %collective-permute-start = (bf16[512,8192]{1,0:T(8,128)(2,1)}, bf16[512,8192]{1,0:T(8,128)(2,1)}, u32[]{:S(2)}, u32[]{:S(2)}) collective-permute-start(bf16[512,8192]{1,0:T(8,128)(2,1)} %bitcast.57), channel_id=1, source_target_pairs={{8,0},{16,8},{24,16},{32,24},{40,32},{48,40},{56,48},{64,56},{72,6... | collective-permute-start | bytes 25165832 | tf_op jit(solution)/shard_map/ppermute | solution.py:14
  378.8 296.2 %all-reduce.7.cloned.1.call-start = ((), (), s32[]{:S(2)}) async-start(), calls=%async_computation.1 | async-start | bytes 262144 | tf_op jit(solution)/shard_map/psum | solution.py:82
  379.8 162.4 %copy-start.4 = (f32[64]{0:T(128)S(1)}, f32[64]{0:T(128)}, u32[]{:S(2)}) copy-start(f32[64]{0:T(128)} %param.16) | copy-start | bytes 772
  551.2 20.1 %copy-start.3 = (f32[8192]{0:T(1024)S(1)}, f32[8192]{0:T(1024)}, u32[]{:S(2)}) copy-start(f32[8192]{0:T(1024)} %param.18) | copy-start | bytes 98308
  585.5 3.2 copy-start.1
  588.8 3.7 copy-start.2
  592.1 218.5 %all-reduce.9.cloned.1.call-start = ((), (), s32[]{:S(2)}) async-start(), calls=%async_computation.2 | async-start | bytes 8388608 | tf_op jit(solution)/shard_map/psum | solution.py:85
Sparse Core Ops, SparseCore 0:
  378.9 163.2 all-reduce.4
  592.2 82.6 all-reduce.6
  681.5 129.0 all-reduce.8
where the time goes:
time: 825 us; the launch traced here: 823 us
  local copies, waits for them, and re-layouts  366 us (44%)
  waiting for transfers between devices  348 us (42%)
  other arithmetic  60.8 us (7%)
  matrix products  32.1 us (4%)
  between operations  14.5 us (2%)
    gather x8, local copies, waits for them, and re-layouts, contact_rows(): far = jnp.take(frame_block, second, axis=2)  284 us
    psum x1, waiting for transfers between devices, local(): latent = jnp.tanh(lax.psum(partial_sum, 'pairs') + enc_bias[:, None])  142 us
    psum x1, waiting for transfers between devices, local(): grad_dec, grad_enc = lax.psum((grad_dec, grad_enc), 'frames')  129 us
    psum x1, waiting for transfers between devices, local(): backward = lax.psum(back_terms, 'pairs')  76.2 us
    reduce_sum x4, other arithmetic, contact_rows(): distance = jnp.sqrt(jnp.sum(offset * offset, axis=1))  26.4 us
    dynamic_update_slice x8, local copies, waits for them, and re-layouts, all_contacts(): lax.map(partial(contact_rows, first_res=first_res, second=second), grouped)  24 us
    gather x1, local copies, waits for them, and re-layouts, later_rows(): jnp.take(following, jnp.maximum(row_ids - frame_rows, 0), axis=0)  20.1 us
    gather x1, local copies, waits for them, and re-layouts, later_rows(): own_part = jnp.take(own, jnp.minimum(row_ids, frame_rows - 1), axis=0)  19.9 us
  transfers between devices with their start and end apart: 4, of which 3 were waited for; matrix products, arithmetic and copies ran while one was open for 5% of the time, Pallas kernels for 0%

commit v1 on v0

--- a/solution.py
+++ b/solution.py
@@ -79,7 +79,7 @@
     zeros = jnp.zeros((latent.shape[0], dec_weight.shape[1]), jnp.float32)
     grad_dec, back_blocks = lax.scan(decode_block, zeros, jnp.arange(block_count, dtype=jnp.int32))
     back_terms = jnp.transpose(back_blocks, (1, 0, 2)).reshape(latent.shape[0], frame_rows)
-    backward = lax.psum(back_terms, "pairs")
+    backward = jnp.sum(lax.all_gather(back_terms, "pairs"), axis=0)
     hidden_bf = (backward * (1.0 - latent * latent)).astype(jnp.bfloat16)
     grad_enc = jnp.dot(hidden_bf, own_contacts, preferred_element_type=jnp.float32)
     grad_dec, grad_enc = lax.psum((grad_dec, grad_enc), "frames")

time: 825 us -> 789 us (0.956)
  waiting for transfers between devices: 348 us -> 310 us
    psum x1 -> x0, waiting for transfers between devices: 76.2 us -> none  [local(): backward = lax.psum(back_terms, 'pairs')]
    all_gather x0 -> x1, waiting for transfers between devices: none -> 37.8 us  [local(): backward = jnp.sum(lax.all_gather(back_terms, 'pairs'), axis=0)]
where the time goes in v1:
time: 789 us; the launch traced here: 787 us
  local copies, waits for them, and re-layouts  366 us (46%)
  waiting for transfers between devices  310 us (39%)
  other arithmetic  62.1 us (8%)
  matrix products  32 us (4%)
  between operations  14.5 us (2%)
    gather x8, local copies, waits for them, and re-layouts, contact_rows(): far = jnp.take(frame_block, second, axis=2)  284 us
    psum x1, waiting for transfers between devices, local(): latent = jnp.tanh(lax.psum(partial_sum, 'pairs') + enc_bias[:, None])  142 us
    psum x1, waiting for transfers between devices, local(): grad_dec, grad_enc = lax.psum((grad_dec, grad_enc), 'frames')  130 us
    all_gather x1, waiting for transfers between devices, local(): backward = jnp.sum(lax.all_gather(back_terms, 'pairs'), axis=0)  37.8 us
    reduce_sum x4, other arithmetic, contact_rows(): distance = jnp.sqrt(jnp.sum(offset * offset, axis=1))  26.4 us
    dynamic_update_slice x8, local copies, waits for them, and re-layouts, all_contacts(): lax.map(partial(contact_rows, first_res=first_res, second=second), grouped)  24 us
    gather x1, local copies, waits for them, and re-layouts, later_rows(): jnp.take(following, jnp.maximum(row_ids - frame_rows, 0), axis=0)  20.1 us
    gather x1, local copies, waits for them, and re-layouts, later_rows(): own_part = jnp.take(own, jnp.minimum(row_ids, frame_rows - 1), axis=0)  19.9 us
  transfers between devices with their start and end apart: 4, of which 3 were waited for; matrix products, arithmetic and copies ran while one was open for 5% of the time, Pallas kernels for 0%

profile of v1, /device:TPU:0, one launch (start us, length us, event | category | flops | bytes accessed | tf_op | source)
XLA Modules:
  0.0 787.0 jit_solution(13970666713779171730)
XLA Ops:
  7.2 363.3 %while.2 = (s32[]{:T(128)}, bf16[4,128,8192]{2,1,0:T(8,128)(2,1)}, s32[8192]{0:T(1024)}, f32[4,128,3,384]{3,1,0,2:T(8,128)}, s32[64]{0:T(128)}, /*index=5*/s32[]{:T(128)}) while((s32[]{:T(128)}, bf16[4,128,8192]{2,1,0:T(8,128)(2,1)}, s32[8192]{0:T(1024)}, f32[4,128,3,384]{3,1,0,2:T(8,128)}, s32[64]{0:T(128)}, /*index=5*/s32[]{:T(128)}) %tuple.40), condition=%wide.region_2.3_spmd, body=%wide.region_0.2_spmd.sunk | while | flops 17933888 | bytes 85054936 | solution.py:31
  9.4 0.8 compare_select_fusion.6
  10.2 1.1 constant_dynamic-slice_fusion.2
  12.5 59.9 %gather_fusion = f32[8192,128,3]{1,2,0:T(4,128)} fusion(f32[128,3,384]{0,1,2:T(4,128)S(1)} %bitcast.55, s32[8192]{0:T(1024)S(1)} %broadcast_clamp_fusion.2), kind=kCustom, calls=%fused_computation.clone.1 | custom fusion | bytes 25198592 | tf_op jit(solution)/shard_map/while/body/eval_jaxpr/jit(_take)/gather | solution.py:19
  72.4 11.1 %copy.28 = f32[128,3,8192]{0,2,1:T(8,128)} copy(f32[128,3,8192]{0,1,2:T(4,128)} %bitcast.56) | data formatting | bytes 25165824 | tf_op jit(solution)/shard_map/while/body/eval_jaxpr/jit(_take)/gather | solution.py:19
  83.5 6.6 multiply_reduce_fusion.2
  90.1 2.0 divide_convert_fusion.2
  92.1 2.9 copy.30
  95.0 3.1 constant_dynamic-update-slice_fusion.2
  100.3 0.8 compare_select_fusion.6
  101.1 1.1 constant_dynamic-slice_fusion.2
  103.3 59.9 %gather_fusion = f32[8192,128,3]{1,2,0:T(4,128)} fusion(f32[128,3,384]{0,1,2:T(4,128)S(1)} %bitcast.55, s32[8192]{0:T(1024)S(1)} %broadcast_clamp_fusion.2), kind=kCustom, calls=%fused_computation.clone.1 | custom fusion | bytes 25198592 | tf_op jit(solution)/shard_map/while/body/eval_jaxpr/jit(_take)/gather | solution.py:19
  163.2 11.1 %copy.28 = f32[128,3,8192]{0,2,1:T(8,128)} copy(f32[128,3,8192]{0,1,2:T(4,128)} %bitcast.56) | data formatting | bytes 25165824 | tf_op jit(solution)/shard_map/while/body/eval_jaxpr/jit(_take)/gather | solution.py:19
  174.3 6.6 multiply_reduce_fusion.2
  180.9 2.0 divide_convert_fusion.2
  183.0 2.9 copy.30
  185.9 3.1 constant_dynamic-update-slice_fusion.2
  191.0 0.8 compare_select_fusion.6
  191.9 1.1 constant_dynamic-slice_fusion.2
  194.1 59.9 %gather_fusion = f32[8192,128,3]{1,2,0:T(4,128)} fusion(f32[128,3,384]{0,1,2:T(4,128)S(1)} %bitcast.55, s32[8192]{0:T(1024)S(1)} %broadcast_clamp_fusion.2), kind=kCustom, calls=%fused_computation.clone.1 | custom fusion | bytes 25198592 | tf_op jit(solution)/shard_map/while/body/eval_jaxpr/jit(_take)/gather | solution.py:19
  254.0 11.1 %copy.28 = f32[128,3,8192]{0,2,1:T(8,128)} copy(f32[128,3,8192]{0,1,2:T(4,128)} %bitcast.56) | data formatting | bytes 25165824 | tf_op jit(solution)/shard_map/while/body/eval_jaxpr/jit(_take)/gather | solution.py:19
  265.1 6.6 multiply_reduce_fusion.2
  271.7 2.0 divide_convert_fusion.2
  273.7 2.9 copy.30
  276.6 3.1 constant_dynamic-update-slice_fusion.2
  282.7 1.1 constant_dynamic-slice_fusion.2
  284.9 59.9 %gather_fusion = f32[8192,128,3]{1,2,0:T(4,128)} fusion(f32[128,3,384]{0,1,2:T(4,128)S(1)} %bitcast.55, s32[8192]{0:T(1024)S(1)} %broadcast_clamp_fusion.2), kind=kCustom, calls=%fused_computation.clone.1 | custom fusion | bytes 25198592 | tf_op jit(solution)/shard_map/while/body/eval_jaxpr/jit(_take)/gather | solution.py:19
  344.8 11.1 %copy.28 = f32[128,3,8192]{0,2,1:T(8,128)} copy(f32[128,3,8192]{0,1,2:T(4,128)} %bitcast.56) | data formatting | bytes 25165824 | tf_op jit(solution)/shard_map/while/body/eval_jaxpr/jit(_take)/gather | solution.py:19
  355.9 6.6 multiply_reduce_fusion.2
  362.5 2.0 divide_convert_fusion.2
  364.6 2.9 copy.30
  367.5 3.1 constant_dynamic-update-slice_fusion.2
  370.5 1.3 collective-permute-start
  371.8 6.9 convolution_bitcast_fusion.1
  379.8 19.9 %gather_fusion.2 = bf16[512,8192]{1,0:T(8,128)(2,1)} fusion(bf16[512,8192]{1,0:T(8,128)(2,1)} %bitcast.60, s32[1024]{0:T(1024)S(1)} %pad_clamp_fusion.2), kind=kCustom, calls=%fused_computation.2.clone | custom fusion | bytes 16779264 | tf_op jit(solution)/shard_map/while/body/eval_jaxpr/jit(_take)/gather | solution.py:36
  399.7 142.4 %all-reduce.4.cloned.1.call-done = f32[64,512]{1,0:T(8,128)} async-done(((f32[64,512]{1,0:T(8,128)}), f32[64,512]{1,0:T(8,128)}) %all-reduce.4.cloned.1.call-update) | async-done | bytes 131088 | tf_op jit(solution)/shard_map/psum | solution.py:51
  542.2 9.1 %fusion.9 = f32[512,8192]{1,0:T(8,128)} fusion(bf16[64,8192]{1,0:T(8,128)(2,1)S(1)} %copy-done, f32[64,512]{1,0:T(8,128)} %all-reduce.4.cloned.1.call-done, f32[64]{0:T(128)S(1)} %copy-done.4), kind=kOutput, calls=%fused_computation.39 | convolution fusion | flops 536936448 | bytes 17957120 | tf_op jit(solution)/shard_map/while/body/eval_jaxpr/dot_general | solution.py:64
  551.2 20.1 %gather_fusion.3 = bf16[512,8192]{1,0:T(8,128)(2,1)} fusion(bf16[512,8192]{1,0:T(8,128)(2,1)} %collective-permute-done, s32[1024]{0:T(1024)S(1)} %pad_clamp_fusion.1), kind=kCustom, calls=%fused_computation.3.clone | custom fusion | bytes 16779264 | tf_op jit(solution)/shard_map/while/body/eval_jaxpr/jit(_take)/gather | solution.py:37
  571.4 14.2 %select_convert_fusion = bf16[512,8192]{1,0:T(8,128)(2,1)S(1)} fusion(f32[512,8192]{1,0:T(8,128)} %fusion.9, bf16[512,8192]{1,0:T(8,128)(2,1)} %gather_fusion.3, bf16[512,8192]{1,0:T(8,128)(2,1)} %gather_fusion.2, f32[]{:T(128)S(6)} %sqrt.15, f32[8192]{0:T(1024)S(1)} %copy-done.3, pred[512]{0:T(512)(128)(4,1)S(1)} %get-tuple-element.89, ...), kind=kLoop, calls=%fused_computation.18 | loop fusion | flops 37748736 | bytes 41977860 | tf_op jit(solution)/shard_map/while/body/eval_jaxpr/convert_element_type | solution.py:72
  585.6 3.2 copy-done.1
  588.8 3.3 convolution_bitcast_fusion
  592.4 6.3 fusion.7
  598.8 37.8 %all-gather.3.cloned.1.call-done = f32[512,512]{1,0:T(8,128)} async-done(((f32[64,512]{1,0:T(8,128)}), f32[512,512]{1,0:T(8,128)}) %all-gather.3.cloned.1.call-update) | async-done | bytes 1048592 | tf_op jit(solution)/shard_map/all_gather | solution.py:82
  636.5 1.3 reduce_sum.18
  637.8 6.3 fusion.2
  644.2 130.1 %all-reduce.6.cloned.1.call-done = (f32[64,8192]{1,0:T(8,128)}, f32[64,8192]{1,0:T(8,128)}) async-done(((f32[64,8192]{1,0:T(8,128)}, f32[64,8192]{1,0:T(8,128)}), (f32[64,8192]{1,0:T(8,128)}, f32[64,8192]{1,0:T(8,128)})) %all-reduce.6.cloned.1.call-update) | async-done | bytes 4194320 | tf_op jit(solution)/shard_map/psum | solution.py:85
  774.3 3.1 copy.44
  777.4 3.1 copy.45
  (60 shorter events, 14.4 us)
Async XLA Ops:
  7.2 535.0 %copy-start = (bf16[64,8192]{1,0:T(8,128)(2,1)S(1)}, bf16[64,8192]{1,0:T(8,128)(2,1)}, u32[]{:S(2)}) copy-start(bf16[64,8192]{1,0:T(8,128)(2,1)} %param.17) | copy-start | bytes 3145732
  7.2 535.0 %all-reduce.4.cloned.1.call-start = ((), (), s32[]{:S(2)}) async-start(), calls=%async_computation | async-start | bytes 262144 | tf_op jit(solution)/shard_map/psum | solution.py:51
  370.5 180.7 %collective-permute-start = (bf16[512,8192]{1,0:T(8,128)(2,1)}, bf16[512,8192]{1,0:T(8,128)(2,1)}, u32[]{:S(2)}, u32[]{:S(2)}) collective-permute-start(bf16[512,8192]{1,0:T(8,128)(2,1)} %bitcast.58), channel_id=1, source_target_pairs={{8,0},{16,8},{24,16},{32,24},{40,32},{48,40},{56,48},{64,56},{72,6... | collective-permute-start | bytes 25165832 | tf_op jit(solution)/shard_map/ppermute | solution.py:14
  378.8 257.7 %all-gather.3.cloned.1.call-start = ((), (), s32[]{:S(2)}) async-start(), calls=%async_computation.1 | async-start | bytes 1179648 | tf_op jit(solution)/shard_map/all_gather | solution.py:82
  379.8 162.4 %copy-start.4 = (f32[64]{0:T(128)S(1)}, f32[64]{0:T(128)}, u32[]{:S(2)}) copy-start(f32[64]{0:T(128)} %param.16) | copy-start | bytes 772
  551.2 20.1 %copy-start.3 = (f32[8192]{0:T(1024)S(1)}, f32[8192]{0:T(1024)}, u32[]{:S(2)}) copy-start(f32[8192]{0:T(1024)} %param.18) | copy-start | bytes 98308
  585.5 3.2 copy-start.1
  588.8 3.7 copy-start.2
  592.1 182.2 %all-reduce.6.cloned.1.call-start = ((), (), s32[]{:S(2)}) async-start(), calls=%async_computation.2 | async-start | bytes 8388608 | tf_op jit(solution)/shard_map/psum | solution.py:85
Sparse Core Ops, SparseCore 0:
  378.9 163.2 all-reduce.3
  592.2 44.2 all-gather.2
  644.3 129.9 all-reduce.5
